TPU v7x, 32 devices: a whole 2x2x4 slice. The times are simulated.
32 devices in a mesh: vol: 4 (over y, x), orient: 4 (over z), dp: 2 (over core).
Axes of the slice: x: 2, y: 2, z: 4, core: 2. Of those that a mesh axis runs over, the one named last changes fastest.
Arguments:
- volume: float32 [128, 65, 2, 8, 128], P('vol'), may hold values from -6 to 6
- weight_bank: float32 [64, 128, 128], replicated, may hold values from -3 to 3
- tile_slab: int32 [128, 65, 1], P(('vol', 'orient')), may hold values from 0 to 3; in each aligned block of 520 rows (0 to 519, 520 to 1039, ..., all dimensions but the last counted through in order) at most 260 rows name the same one
- tile_plane: int32 [128, 65], P(('vol', 'orient')), may hold values from 0 to 31
- tile_weight: int32 [128, 65], P(('vol', 'orient')), may hold values from 0 to 63
- particles: float32 [256, 65, 2, 128], P('dp'), may hold values from -6 to 6
- ctf: float32 [256, 65, 128], P('dp'), may hold values from -1 to 1
- noise_weight: float32 [65, 128], replicated, may hold values from 0.002 to 0.11
- offsets: int32 [256, 2], P('dp'), may hold values from -3 to 3
- earlier_class: int32 [256], P('dp'), may hold values from 0 to 7
- pose_free_term: float32 [256], P('dp'), may hold values from -160 to 160
Outputs:
- numerator: float32 [128, 65, 3, 8, 128], P(('vol', 'orient', 'dp'))
- posterior: float32 [256, 8], P('dp')
- log_evidence: float32 [256], P('dp')
Inputs may be any that keep to these rules, and one draw needn't show every extreme that they name: `tile_slab`: among the 65 tiles of the 8 poses of one device at most 260 name one slab, and in every draw some device's tiles name some slab exactly 260 times.
All inputs are finite; a program needn't handle non-finite values.
Results may differ from a plain program's by a relative error of at most 0.0003.
Values sent between devices are 32-bit elements; how exact they have to be, the bound alone decides.
No kernel may reach another device: no remote copies, remote signals or barrier semaphores. Data moves between devices by JAX's collectives and lax.ppermute only.
A program may use at most 192 MiB of HBM per device.

v0:
```python
import math

import jax
import jax.numpy as jnp
from jax import lax
from jax.sharding import PartitionSpec as P

SIDE = 128
NTRANS = 9


PREVIOUS_REWARD = 1.5
PRECISE = lax.Precision.HIGHEST


def pixel_frequencies(image_side, tile_count, tile_width):
    pixel = jnp.arange(tile_count * tile_width, dtype=jnp.int32).reshape(tile_count, tile_width)
    half_width = image_side // 2 + 1
    freq_x = pixel % half_width
    row_index = pixel // half_width
    freq_y = jnp.where(row_index < image_side // 2, row_index, row_index - image_side)
    return (freq_x, freq_y)


def moved_images(images, offsets, freq_x, freq_y, image_side, trans_step):
    shift_horizontal = offsets[:, 0] + (trans_step % 3 - 1)
    move_y = offsets[:, 1] + (trans_step // 3 - 1)
    turns = jnp.mod(
        freq_x[None] * shift_horizontal[:, None, None] + freq_y[None] * move_y[:, None, None],
        image_side,
    )
    phase_angle = turns.astype(jnp.float32) * (2.0 * math.pi / image_side)
    cosine = jnp.cos(phase_angle)
    sine_part = jnp.sin(phase_angle)
    real_part = images[:, :, 0, :]
    imag_part = images[:, :, 1, :]
    return jnp.stack(
        [real_part * cosine + imag_part * sine_part, imag_part * cosine - real_part * sine_part],
        axis=2,
    )


def project_tiles(blocks, weight_bank, chosen):
    matrices = weight_bank[chosen]
    return jnp.einsum("nckr,nrq->nckq", blocks, matrices, precision=PRECISE)


def back_project(tile_rows, weight_bank, chosen):
    matrices = weight_bank[chosen]
    return jnp.einsum("nmkq,nrq->nmkr", tile_rows, matrices, precision=PRECISE)


def shards(
    volume,
    weight_bank,
    tile_slab,
    tile_plane,
    tile_weight,
    particles,
    ctf,
    noise_weight,
    offsets,
    earlier_class,
    pose_free_term,
):
    slab_count = lax.axis_size("vol")
    pose_local = tile_plane.shape[0]
    tile_count = tile_plane.shape[1]
    tile_width = particles.shape[3]
    class_labels = volume.shape[3]
    planes = volume.shape[0]
    capacity = max(2, 2 * pose_local * tile_count // slab_count)
    row_total = pose_local * tile_count
    slab_of = tile_slab[:, :, 0].reshape(row_total)
    plane_of = tile_plane.reshape(row_total)
    chosen = tile_weight.reshape(row_total)
    target = (slab_of[:, None] == jnp.arange(slab_count, dtype=jnp.int32)[None]).astype(jnp.int32)
    slot_rank = jnp.sum((jnp.cumsum(target, axis=0) - 1) * target, axis=1)
    slot_index = slab_of * capacity + slot_rank
    local_cell = plane_of * tile_count + jnp.tile(
        jnp.arange(tile_count, dtype=jnp.int32), pose_local
    )
    request = jnp.full((slab_count * capacity,), -1, jnp.int32).at[slot_index].set(local_cell)
    request = request.reshape(slab_count, capacity)
    flat_volume = volume.reshape(planes * tile_count, 2, class_labels, tile_width)

    def project_group(item_pair):
        return project_tiles(item_pair[0], weight_bank, item_pair[1])

    def spread_group(item_pair):
        return back_project(item_pair[0], weight_bank, item_pair[1])

    weight_request = jnp.zeros((slab_count * capacity,), jnp.int32).at[slot_index].set(chosen)
    weight_request = weight_request.reshape(slab_count, capacity)
    incoming, incoming_weight = (
        lax.all_to_all(request, "vol", split_axis=0, concat_axis=0, tiled=True),
        lax.all_to_all(weight_request, "vol", split_axis=0, concat_axis=0, tiled=True),
    )
    is_valid = incoming >= 0
    picked = flat_volume[jnp.maximum(incoming, 0)]
    blocks = jnp.where(is_valid[..., None, None, None], picked, 0.0)
    pieces = lax.map(project_group, (blocks, incoming_weight))
    returned = lax.all_to_all(pieces, "vol", split_axis=0, concat_axis=0, tiled=True)
    slices = returned.reshape(slab_count * capacity, 2, class_labels, tile_width)[slot_index]
    slices = slices.reshape(pose_local, tile_count, 2, class_labels, tile_width)
    freq_x, freq_y = pixel_frequencies(SIDE, tile_count, tile_width)
    ctf_noise = noise_weight[None] * ctf
    power = jnp.sum(slices * slices, axis=2)
    norm_term = jnp.einsum("itq,ptkq->ikp", ctf_noise * ctf, power, precision=PRECISE)
    trans_steps = jnp.arange(NTRANS, dtype=jnp.int32)

    def score_step(trans_step):
        moved = moved_images(particles, offsets, freq_x, freq_y, SIDE, trans_step)
        return jnp.einsum(
            "itcq,ptckq->ikp", ctf_noise[:, :, None, :] * moved, slices, precision=PRECISE
        )

    cross_term = lax.map(score_step, trans_steps)
    earlier_class_term = jnp.where(
        earlier_class[:, None] == jnp.arange(class_labels, dtype=jnp.int32)[None],
        PREVIOUS_REWARD,
        0.0,
    )
    earlier_class_term = earlier_class_term + pose_free_term[:, None]
    scores = 2.0 * cross_term - norm_term[None] + earlier_class_term[None, :, :, None]
    peak_value = lax.pmax(jnp.max(scores, axis=(0, 2, 3)), ("vol", "orient"))
    exp_scores = jnp.exp(scores - peak_value[None, :, None, None])
    class_mass = lax.psum(jnp.sum(exp_scores, axis=(0, 3)), ("vol", "orient"))
    mass_total = jnp.sum(class_mass, axis=1)
    posterior = class_mass / mass_total[:, None]
    evidence = peak_value + jnp.log(mass_total)
    pose_count = pose_local * lax.axis_size("vol") * lax.axis_size("orient")
    post_share = exp_scores * (pose_count / mass_total)[None, :, None, None]

    def add_step(running, item_pair):
        trans_step, share_step = item_pair
        moved = moved_images(particles, offsets, freq_x, freq_y, SIDE, trans_step)
        term = jnp.einsum(
            "ikp,itcq->ptckq", share_step, ctf[:, :, None, :] * moved, precision=PRECISE
        )
        return (running + term, None)

    start = jnp.zeros((pose_local, tile_count, 2, class_labels, tile_width), jnp.float32)
    data_rows = lax.scan(add_step, start, (trans_steps, post_share))[0]
    weight_rows = jnp.einsum(
        "ikp,itq->ptkq", jnp.sum(post_share, axis=0), ctf * ctf, precision=PRECISE
    )
    slice_rows = jnp.concatenate([data_rows, weight_rows[:, :, None]], axis=2)
    outgoing = jnp.zeros((slab_count * capacity, 3, class_labels, tile_width), jnp.float32)
    outgoing = outgoing.at[slot_index].set(
        slice_rows.reshape(row_total, 3, class_labels, tile_width)
    )
    outgoing = outgoing.reshape(slab_count, capacity, 3, class_labels, tile_width)
    arrived_rows = lax.all_to_all(outgoing, "vol", split_axis=0, concat_axis=0, tiled=True)
    arrived = lax.map(spread_group, (arrived_rows, incoming_weight))
    cell_index = jnp.maximum(incoming, 0).reshape(-1)
    accumulated = jnp.zeros((planes * tile_count, 3, class_labels, tile_width), jnp.float32)
    accumulated = accumulated.at[cell_index].add(arrived.reshape(-1, 3, class_labels, tile_width))
    accumulated = accumulated.reshape(planes, tile_count, 3, class_labels, tile_width)
    numerator = lax.psum_scatter(accumulated, ("orient", "dp"), scatter_dimension=0, tiled=True)
    return (numerator, posterior, evidence)


def solution(mesh):
    in_specs = (
        P("vol", None, None, None, None),
        P(),
        P(("vol", "orient"), None, None),
        P(("vol", "orient"), None),
        P(("vol", "orient"), None),
        P("dp", None, None, None),
        P("dp", None, None),
        P(),
        P("dp", None),
        P("dp"),
        P("dp"),
    )
    out_specs = (P(("vol", "orient", "dp"), None, None, None, None), P("dp", None), P("dp"))
    return jax.shard_map(shards, mesh=mesh, in_specs=in_specs, out_specs=out_specs, check_vma=False)
```

profile of v0, /device:TPU:0, one launch (start us, length us, event | category | flops | bytes accessed | tf_op | source)
XLA Modules:
  0.0 1770.1 jit_solution(17040077565508846166)
XLA Ops:
  31.7 13.2 gather_fusion.2
  52.4 130.6 %while.52 = (s32[]{:T(128)}, f32[4,260,2,8,128]{4,3,2,1,0:T(8,128)}, f32[4,260,2,8,128]{4,3,2,1,0:T(8,128)}, s32[4,260]{1,0:T(4,128)S(1)}, f32[64,128,128]{2,1,0:T(8,128)}) while((s32[]{:T(128)}, f32[4,260,2,8,128]{4,3,2,1,0:T(8,128)}, f32[4,260,2,8,128]{4,3,2,1,0:T(8,128)}, s32[4,260]{1,0:T(4,128)S(1)}, ...), condition=%wide.region_6.7_spmd.clone, body=%wide.region_5.6_spmd.sunk.clone | while | flops 817891072 | bytes 55387264 | solution.py:102
  52.5 14.8 gather_fusion
  67.2 17.9 %bitcast_dynamic-update-slice_fusion.6 = f32[4,260,2,8,128]{4,3,2,1,0:T(8,128)} fusion(f32[4,260,2,8,128]{4,3,2,1,0:T(8,128)} %get-tuple-element.798, s32[]{:T(128)} %get-tuple-element.797, f32[260,128,128]{2,1,0:T(8,128)} %gather_fusion, f32[4,260,2,8,128]{4,3,2,1,0:T(8,128)} %get-tuple-element.804), kind=kOutput, calls=%fused_computation.78.clone.1.clone | convolution fusion | flops 817889280 | bytes 21300224 | tf_op jit(solution)/shard_map/while/body/eval_jaxpr/nckr,nrq->nckq/dot_general | solution.py:45
  85.2 14.7 gather_fusion
  99.8 17.9 %bitcast_dynamic-update-slice_fusion.6 = f32[4,260,2,8,128]{4,3,2,1,0:T(8,128)} fusion(f32[4,260,2,8,128]{4,3,2,1,0:T(8,128)} %get-tuple-element.798, s32[]{:T(128)} %get-tuple-element.797, f32[260,128,128]{2,1,0:T(8,128)} %gather_fusion, f32[4,260,2,8,128]{4,3,2,1,0:T(8,128)} %get-tuple-element.804), kind=kOutput, calls=%fused_computation.78.clone.1.clone | convolution fusion | flops 817889280 | bytes 21300224 | tf_op jit(solution)/shard_map/while/body/eval_jaxpr/nckr,nrq->nckq/dot_general | solution.py:45
  117.7 14.7 gather_fusion
  132.5 17.9 %bitcast_dynamic-update-slice_fusion.6 = f32[4,260,2,8,128]{4,3,2,1,0:T(8,128)} fusion(f32[4,260,2,8,128]{4,3,2,1,0:T(8,128)} %get-tuple-element.798, s32[]{:T(128)} %get-tuple-element.797, f32[260,128,128]{2,1,0:T(8,128)} %gather_fusion, f32[4,260,2,8,128]{4,3,2,1,0:T(8,128)} %get-tuple-element.804), kind=kOutput, calls=%fused_computation.78.clone.1.clone | convolution fusion | flops 817889280 | bytes 21300224 | tf_op jit(solution)/shard_map/while/body/eval_jaxpr/nckr,nrq->nckq/dot_general | solution.py:45
  150.4 14.8 gather_fusion
  165.1 17.9 %bitcast_dynamic-update-slice_fusion.6 = f32[4,260,2,8,128]{4,3,2,1,0:T(8,128)} fusion(f32[4,260,2,8,128]{4,3,2,1,0:T(8,128)} %get-tuple-element.798, s32[]{:T(128)} %get-tuple-element.797, f32[260,128,128]{2,1,0:T(8,128)} %gather_fusion, f32[4,260,2,8,128]{4,3,2,1,0:T(8,128)} %get-tuple-element.804), kind=kOutput, calls=%fused_computation.78.clone.1.clone | convolution fusion | flops 817889280 | bytes 21300224 | tf_op jit(solution)/shard_map/while/body/eval_jaxpr/nckr,nrq->nckq/dot_general | solution.py:45
  207.6 75.7 %all-to-all-done.2 = f32[4,260,2,8,128]{4,3,2,1,0:T(8,128)} async-done(((f32[4,260,2,8,128]{4,3,2,1,0:T(8,128)}), f32[4,260,2,8,128]{4,3,2,1,0:T(8,128)}, u32[]{:S(2)}, u32[]{:S(2)}) %all-to-all-start.2) | async-done | bytes 8519712 | tf_op jit(solution)/shard_map/all_to_all | solution.py:103
  295.4 283.1 %while.54 = (s32[]{:T(128)}, f32[9,128,8,8]{1,3,2,0:T(8,128)S(1)}, f32[128,65,128]{2,0,1:T(8,128)}, f32[128,65,2,128]{3,0,1,2:T(8,128)}, s32[128,2]{0,1:T(2,128)...) while((s32[]{:T(128)}, f32[9,128,8,8]{1,3,2,0:T(8,128)S(1)}, ...), condition=%wide.region_8.9_spmd.clone.clone, body=%wide.region_7.8_spmd.clone.sunk.clone | while | flops 1663609216 | bytes 68392240 | solution.py:118
  298.1 19.7 %multiply_add_fusion.8 = (f32[128,65,1,128]{3,0,1,2:T(8,128)S(1)}, f32[128,65,1,128]{3,0,1,2:T(8,128)S(1)}) fusion(f32[128,65,2,128]{3,0,1,2:T(8,128)} %get-tuple-element.828, s32[128]{0:T(128)S(1)} %get-tuple-element.740, s32[65,128]{1,0:T(8,128)S(1)} %get-tuple-element.741, s32[128]{0:T(128)S(1)} %get-tuple-element.742, ...), kind=kLoop, calls=%fused_computation.24.clone.1.clone | loop fusion | flops 23429120 | bytes 17106944 | tf_op jit(solution)/shard_map/while/body/eval_jaxpr/add | solution.py:38
  329.5 19.7 %multiply_add_fusion.8 = (f32[128,65,1,128]{3,0,1,2:T(8,128)S(1)}, f32[128,65,1,128]{3,0,1,2:T(8,128)S(1)}) fusion(f32[128,65,2,128]{3,0,1,2:T(8,128)} %get-tuple-element.828, s32[128]{0:T(128)S(1)} %get-tuple-element.740, s32[65,128]{1,0:T(8,128)S(1)} %get-tuple-element.741, s32[128]{0:T(128)S(1)} %get-tuple-element.742, ...), kind=kLoop, calls=%fused_computation.24.clone.1.clone | loop fusion | flops 23429120 | bytes 17106944 | tf_op jit(solution)/shard_map/while/body/eval_jaxpr/add | solution.py:38
  360.9 19.7 %multiply_add_fusion.8 = (f32[128,65,1,128]{3,0,1,2:T(8,128)S(1)}, f32[128,65,1,128]{3,0,1,2:T(8,128)S(1)}) fusion(f32[128,65,2,128]{3,0,1,2:T(8,128)} %get-tuple-element.828, s32[128]{0:T(128)S(1)} %get-tuple-element.740, s32[65,128]{1,0:T(8,128)S(1)} %get-tuple-element.741, s32[128]{0:T(128)S(1)} %get-tuple-element.742, ...), kind=kLoop, calls=%fused_computation.24.clone.1.clone | loop fusion | flops 23429120 | bytes 17106944 | tf_op jit(solution)/shard_map/while/body/eval_jaxpr/add | solution.py:38
  392.4 19.7 %multiply_add_fusion.8 = (f32[128,65,1,128]{3,0,1,2:T(8,128)S(1)}, f32[128,65,1,128]{3,0,1,2:T(8,128)S(1)}) fusion(f32[128,65,2,128]{3,0,1,2:T(8,128)} %get-tuple-element.828, s32[128]{0:T(128)S(1)} %get-tuple-element.740, s32[65,128]{1,0:T(8,128)S(1)} %get-tuple-element.741, s32[128]{0:T(128)S(1)} %get-tuple-element.742, ...), kind=kLoop, calls=%fused_computation.24.clone.1.clone | loop fusion | flops 23429120 | bytes 17106944 | tf_op jit(solution)/shard_map/while/body/eval_jaxpr/add | solution.py:38
  423.8 19.7 %multiply_add_fusion.8 = (f32[128,65,1,128]{3,0,1,2:T(8,128)S(1)}, f32[128,65,1,128]{3,0,1,2:T(8,128)S(1)}) fusion(f32[128,65,2,128]{3,0,1,2:T(8,128)} %get-tuple-element.828, s32[128]{0:T(128)S(1)} %get-tuple-element.740, s32[65,128]{1,0:T(8,128)S(1)} %get-tuple-element.741, s32[128]{0:T(128)S(1)} %get-tuple-element.742, ...), kind=kLoop, calls=%fused_computation.24.clone.1.clone | loop fusion | flops 23429120 | bytes 17106944 | tf_op jit(solution)/shard_map/while/body/eval_jaxpr/add | solution.py:38
  455.3 19.7 %multiply_add_fusion.8 = (f32[128,65,1,128]{3,0,1,2:T(8,128)S(1)}, f32[128,65,1,128]{3,0,1,2:T(8,128)S(1)}) fusion(f32[128,65,2,128]{3,0,1,2:T(8,128)} %get-tuple-element.828, s32[128]{0:T(128)S(1)} %get-tuple-element.740, s32[65,128]{1,0:T(8,128)S(1)} %get-tuple-element.741, s32[128]{0:T(128)S(1)} %get-tuple-element.742, ...), kind=kLoop, calls=%fused_computation.24.clone.1.clone | loop fusion | flops 23429120 | bytes 17106944 | tf_op jit(solution)/shard_map/while/body/eval_jaxpr/add | solution.py:38
  486.7 19.7 %multiply_add_fusion.8 = (f32[128,65,1,128]{3,0,1,2:T(8,128)S(1)}, f32[128,65,1,128]{3,0,1,2:T(8,128)S(1)}) fusion(f32[128,65,2,128]{3,0,1,2:T(8,128)} %get-tuple-element.828, s32[128]{0:T(128)S(1)} %get-tuple-element.740, s32[65,128]{1,0:T(8,128)S(1)} %get-tuple-element.741, s32[128]{0:T(128)S(1)} %get-tuple-element.742, ...), kind=kLoop, calls=%fused_computation.24.clone.1.clone | loop fusion | flops 23429120 | bytes 17106944 | tf_op jit(solution)/shard_map/while/body/eval_jaxpr/add | solution.py:38
  518.1 19.7 %multiply_add_fusion.8 = (f32[128,65,1,128]{3,0,1,2:T(8,128)S(1)}, f32[128,65,1,128]{3,0,1,2:T(8,128)S(1)}) fusion(f32[128,65,2,128]{3,0,1,2:T(8,128)} %get-tuple-element.828, s32[128]{0:T(128)S(1)} %get-tuple-element.740, s32[65,128]{1,0:T(8,128)S(1)} %get-tuple-element.741, s32[128]{0:T(128)S(1)} %get-tuple-element.742, ...), kind=kLoop, calls=%fused_computation.24.clone.1.clone | loop fusion | flops 23429120 | bytes 17106944 | tf_op jit(solution)/shard_map/while/body/eval_jaxpr/add | solution.py:38
  549.6 19.7 %multiply_add_fusion.8 = (f32[128,65,1,128]{3,0,1,2:T(8,128)S(1)}, f32[128,65,1,128]{3,0,1,2:T(8,128)S(1)}) fusion(f32[128,65,2,128]{3,0,1,2:T(8,128)} %get-tuple-element.828, s32[128]{0:T(128)S(1)} %get-tuple-element.740, s32[65,128]{1,0:T(8,128)S(1)} %get-tuple-element.741, s32[128]{0:T(128)S(1)} %get-tuple-element.742, ...), kind=kLoop, calls=%fused_computation.24.clone.1.clone | loop fusion | flops 23429120 | bytes 17106944 | tf_op jit(solution)/shard_map/while/body/eval_jaxpr/add | solution.py:38
  585.5 40.6 %pmax.7 = f32[128]{0:T(128)S(1)} all-reduce(f32[128]{0:T(128)S(1)} %fusion.84), channel_id=1, replica_groups=mesh['vol'=4,'orient'=4,'dp'=2] {'vol','orient'}, use_global_device_ids=true, to_apply=%region_11.12 | all-reduce | flops 128 | bytes 1024 | tf_op jit(solution)/shard_map/pmax | solution.py:126
  626.1 36.7 %psum.7 = f32[128,8]{0,1:T(8,128)S(1)} all-reduce(f32[128,8]{0,1:T(8,128)S(1)} %fusion.83), channel_id=1, replica_groups=mesh['vol'=4,'orient'=4,'dp'=2] {'vol','orient'}, use_global_device_ids=true, to_apply=%region_13.14 | all-reduce | flops 1024 | bytes 8192 | tf_op jit(solution)/shard_map/psum | solution.py:128
  663.6 299.8 %while.55 = (s32[]{:T(128)}, f32[8,65,2,8,128]{4,0,3,2,1:T(8,128)}, f32[128,65,128]{2,0,1:T(8,128)}, f32[128,65,2,128]{3,0,2,1:T(8,128)}, s32[128,2]{0,1:T(2,128...) while((s32[]{:T(128)}, f32[8,65,2,8,128]{4,0,3,2,1:T(8,128)}, ...), condition=%wide.region_16.17_spmd.clone.clone, body=%wide.region_15.16_spmd.clone.sunk.clone | while | flops 1665739136 | bytes 38507784 | solution.py:144
  665.9 20.7 %multiply_add_fusion.9 = (f32[128,65,1,128]{3,0,2,1:T(8,128)}, f32[128,65,1,128]{3,0,2,1:T(8,128)}) fusion(f32[128,65,2,128]{3,0,2,1:T(8,128)} %get-tuple-element.855, s32[128]{0:T(128)S(1)} %get-tuple-element.771, s32[65,128]{1,0:T(8,128)S(1)} %get-tuple-element.772, s32[128]{0:T(128)S(1)} %get-tuple-element.773, ...), kind=kLoop, calls=%fused_computation.56.clone.1.clone | loop fusion | flops 23429120 | bytes 17106944 | tf_op jit(solution)/shard_map/while/body/eval_jaxpr/add | solution.py:38
  698.6 20.7 %multiply_add_fusion.9 = (f32[128,65,1,128]{3,0,2,1:T(8,128)}, f32[128,65,1,128]{3,0,2,1:T(8,128)}) fusion(f32[128,65,2,128]{3,0,2,1:T(8,128)} %get-tuple-element.855, s32[128]{0:T(128)S(1)} %get-tuple-element.771, s32[65,128]{1,0:T(8,128)S(1)} %get-tuple-element.772, s32[128]{0:T(128)S(1)} %get-tuple-element.773, ...), kind=kLoop, calls=%fused_computation.56.clone.1.clone | loop fusion | flops 23429120 | bytes 17106944 | tf_op jit(solution)/shard_map/while/body/eval_jaxpr/add | solution.py:38
  719.3 10.4 bitcast_add_fusion.3
  732.0 20.7 %multiply_add_fusion.9 = (f32[128,65,1,128]{3,0,2,1:T(8,128)}, f32[128,65,1,128]{3,0,2,1:T(8,128)}) fusion(f32[128,65,2,128]{3,0,2,1:T(8,128)} %get-tuple-element.855, s32[128]{0:T(128)S(1)} %get-tuple-element.771, s32[65,128]{1,0:T(8,128)S(1)} %get-tuple-element.772, s32[128]{0:T(128)S(1)} %get-tuple-element.773, ...), kind=kLoop, calls=%fused_computation.56.clone.1.clone | loop fusion | flops 23429120 | bytes 17106944 | tf_op jit(solution)/shard_map/while/body/eval_jaxpr/add | solution.py:38
  752.7 10.4 bitcast_add_fusion.3
  765.4 20.7 %multiply_add_fusion.9 = (f32[128,65,1,128]{3,0,2,1:T(8,128)}, f32[128,65,1,128]{3,0,2,1:T(8,128)}) fusion(f32[128,65,2,128]{3,0,2,1:T(8,128)} %get-tuple-element.855, s32[128]{0:T(128)S(1)} %get-tuple-element.771, s32[65,128]{1,0:T(8,128)S(1)} %get-tuple-element.772, s32[128]{0:T(128)S(1)} %get-tuple-element.773, ...), kind=kLoop, calls=%fused_computation.56.clone.1.clone | loop fusion | flops 23429120 | bytes 17106944 | tf_op jit(solution)/shard_map/while/body/eval_jaxpr/add | solution.py:38
  798.8 20.7 %multiply_add_fusion.9 = (f32[128,65,1,128]{3,0,2,1:T(8,128)}, f32[128,65,1,128]{3,0,2,1:T(8,128)}) fusion(f32[128,65,2,128]{3,0,2,1:T(8,128)} %get-tuple-element.855, s32[128]{0:T(128)S(1)} %get-tuple-element.771, s32[65,128]{1,0:T(8,128)S(1)} %get-tuple-element.772, s32[128]{0:T(128)S(1)} %get-tuple-element.773, ...), kind=kLoop, calls=%fused_computation.56.clone.1.clone | loop fusion | flops 23429120 | bytes 17106944 | tf_op jit(solution)/shard_map/while/body/eval_jaxpr/add | solution.py:38
  832.2 20.7 %multiply_add_fusion.9 = (f32[128,65,1,128]{3,0,2,1:T(8,128)}, f32[128,65,1,128]{3,0,2,1:T(8,128)}) fusion(f32[128,65,2,128]{3,0,2,1:T(8,128)} %get-tuple-element.855, s32[128]{0:T(128)S(1)} %get-tuple-element.771, s32[65,128]{1,0:T(8,128)S(1)} %get-tuple-element.772, s32[128]{0:T(128)S(1)} %get-tuple-element.773, ...), kind=kLoop, calls=%fused_computation.56.clone.1.clone | loop fusion | flops 23429120 | bytes 17106944 | tf_op jit(solution)/shard_map/while/body/eval_jaxpr/add | solution.py:38
  865.6 20.7 %multiply_add_fusion.9 = (f32[128,65,1,128]{3,0,2,1:T(8,128)}, f32[128,65,1,128]{3,0,2,1:T(8,128)}) fusion(f32[128,65,2,128]{3,0,2,1:T(8,128)} %get-tuple-element.855, s32[128]{0:T(128)S(1)} %get-tuple-element.771, s32[65,128]{1,0:T(8,128)S(1)} %get-tuple-element.772, s32[128]{0:T(128)S(1)} %get-tuple-element.773, ...), kind=kLoop, calls=%fused_computation.56.clone.1.clone | loop fusion | flops 23429120 | bytes 17106944 | tf_op jit(solution)/shard_map/while/body/eval_jaxpr/add | solution.py:38
  898.9 20.7 %multiply_add_fusion.9 = (f32[128,65,1,128]{3,0,2,1:T(8,128)}, f32[128,65,1,128]{3,0,2,1:T(8,128)}) fusion(f32[128,65,2,128]{3,0,2,1:T(8,128)} %get-tuple-element.855, s32[128]{0:T(128)S(1)} %get-tuple-element.771, s32[65,128]{1,0:T(8,128)S(1)} %get-tuple-element.772, s32[128]{0:T(128)S(1)} %get-tuple-element.773, ...), kind=kLoop, calls=%fused_computation.56.clone.1.clone | loop fusion | flops 23429120 | bytes 17106944 | tf_op jit(solution)/shard_map/while/body/eval_jaxpr/add | solution.py:38
  932.3 20.7 %multiply_add_fusion.9 = (f32[128,65,1,128]{3,0,2,1:T(8,128)}, f32[128,65,1,128]{3,0,2,1:T(8,128)}) fusion(f32[128,65,2,128]{3,0,2,1:T(8,128)} %get-tuple-element.855, s32[128]{0:T(128)S(1)} %get-tuple-element.771, s32[65,128]{1,0:T(8,128)S(1)} %get-tuple-element.772, s32[128]{0:T(128)S(1)} %get-tuple-element.773, ...), kind=kLoop, calls=%fused_computation.56.clone.1.clone | loop fusion | flops 23429120 | bytes 17106944 | tf_op jit(solution)/shard_map/while/body/eval_jaxpr/add | solution.py:38
  977.8 69.5 %scatter_fusion = f32[1040,3,8,128]{3,2,1,0:T(8,128)} fusion(f32[1040,3,8,128]{3,2,1,0:T(8,128)} %broadcast_in_dim.61, s32[520]{0:T(1024)S(1)} %fusion.92, f32[520,3,8,128]{3,2,1,0:T(8,128)} %pad_maximum_fusion), kind=kCustom, calls=%fused_computation.6 | custom fusion | bytes 19171360 | tf_op jit(solution)/shard_map/scatter | solution.py:150
  1053.8 124.7 %all-to-all-done.3 = f32[4,260,3,8,128]{4,3,2,1,0:T(8,128)} async-done(((f32[4,260,3,8,128]{4,3,2,1,0:T(8,128)}), f32[4,260,3,8,128]{4,3,2,1,0:T(8,128)}, u32[]{:S(2)}, u32[]{:S(2)}) %all-to-all-start.3) | async-done | bytes 12779552 | tf_op jit(solution)/shard_map/all_to_all | solution.py:154
  1178.5 182.9 %while.53 = (s32[]{:T(128)}, f32[4,260,3,8,128]{4,3,2,1,0:T(8,128)}, f32[4,260,3,8,128]{4,3,2,1,0:T(8,128)}, s32[4,260]{1,0:T(4,128)}, f32[64,128,128]{2,1,0:T(8,128)}) while((s32[]{:T(128)}, f32[4,260,3,8,128]{4,3,2,1,0:T(8,128)}, f32[4,260,3,8,128]{4,3,2,1,0:T(8,128)}, s32[4,260]{1,0:T(4,128)}, ...), condition=%wide.region_20.21_spmd.clone, body=%wide.region_19.20_spmd.sunk.clone | while | flops 1226835712 | bytes 57517184 | solution.py:155
  1179.5 14.8 gather_fusion.1
  1194.2 30.2 %bitcast_dynamic-update-slice_fusion.7 = f32[4,260,3,8,128]{4,3,2,1,0:T(8,128)} fusion(f32[4,260,3,8,128]{4,3,2,1,0:T(8,128)} %get-tuple-element.867, s32[]{:T(128)} %get-tuple-element.866, f32[260,128,128]{2,1,0:T(8,128)} %gather_fusion.1, f32[4,260,3,8,128]{4,3,2,1,0:T(8,128)} %get-tuple-element.873), kind=kOutput, calls=%fused_computation.87.clone.1.clone | convolution fusion | flops 1226833920 | bytes 23430144 | tf_op jit(solution)/shard_map/while/body/eval_jaxpr/nmkq,nrq->nmkr/dot_general | solution.py:50
  1225.2 14.7 gather_fusion.1
  1239.8 30.2 %bitcast_dynamic-update-slice_fusion.7 = f32[4,260,3,8,128]{4,3,2,1,0:T(8,128)} fusion(f32[4,260,3,8,128]{4,3,2,1,0:T(8,128)} %get-tuple-element.867, s32[]{:T(128)} %get-tuple-element.866, f32[260,128,128]{2,1,0:T(8,128)} %gather_fusion.1, f32[4,260,3,8,128]{4,3,2,1,0:T(8,128)} %get-tuple-element.873), kind=kOutput, calls=%fused_computation.87.clone.1.clone | convolution fusion | flops 1226833920 | bytes 23430144 | tf_op jit(solution)/shard_map/while/body/eval_jaxpr/nmkq,nrq->nmkr/dot_general | solution.py:50
  1270.8 14.7 gather_fusion.1
  1285.5 30.2 %bitcast_dynamic-update-slice_fusion.7 = f32[4,260,3,8,128]{4,3,2,1,0:T(8,128)} fusion(f32[4,260,3,8,128]{4,3,2,1,0:T(8,128)} %get-tuple-element.867, s32[]{:T(128)} %get-tuple-element.866, f32[260,128,128]{2,1,0:T(8,128)} %gather_fusion.1, f32[4,260,3,8,128]{4,3,2,1,0:T(8,128)} %get-tuple-element.873), kind=kOutput, calls=%fused_computation.87.clone.1.clone | convolution fusion | flops 1226833920 | bytes 23430144 | tf_op jit(solution)/shard_map/while/body/eval_jaxpr/nmkq,nrq->nmkr/dot_general | solution.py:50
  1316.4 14.8 gather_fusion.1
  1331.2 30.2 %bitcast_dynamic-update-slice_fusion.7 = f32[4,260,3,8,128]{4,3,2,1,0:T(8,128)} fusion(f32[4,260,3,8,128]{4,3,2,1,0:T(8,128)} %get-tuple-element.867, s32[]{:T(128)} %get-tuple-element.866, f32[260,128,128]{2,1,0:T(8,128)} %gather_fusion.1, f32[4,260,3,8,128]{4,3,2,1,0:T(8,128)} %get-tuple-element.873), kind=kOutput, calls=%fused_computation.87.clone.1.clone | convolution fusion | flops 1226833920 | bytes 23430144 | tf_op jit(solution)/shard_map/while/body/eval_jaxpr/nmkq,nrq->nmkr/dot_general | solution.py:50
  1370.1 141.5 %scatter_fusion.1 = f32[2080,3,8,128]{3,2,1,0:T(8,128)} fusion(f32[2080,3,8,128]{3,2,1,0:T(8,128)} %broadcast_in_dim.53, s32[1040]{0:T(1024)S(1)} %copy-done.7, f32[1040,3,8,128]{3,2,1,0:T(8,128)} %bitcast.202), kind=kCustom, calls=%fused_computation.7 | custom fusion | flops 3194880 | bytes 38342720 | tf_op jit(solution)/shard_map/scatter-add | solution.py:158
  1512.9 250.1 %reduce-scatter.2.cloned.1.call-done = f32[4,65,3,8,128]{4,3,2,1,0:T(8,128)} async-done(((f32[32,65,3,8,128]{4,3,2,1,0:T(8,128)}), f32[4,65,3,8,128]{4,3,2,1,0:T(8,128)}) %reduce-scatter.2.cloned.1.call-update) | async-done | bytes 3194896 | tf_op jit(solution)/shard_map/reduce_scatter | solution.py:160
  (228 shorter events, 275.1 us)
Async XLA Ops:
  16.5 10.7 all-to-all-start
  27.2 25.3 %all-to-all-start.1 = ((s32[4,1,260]{2,1,0:T(1,128)}), s32[4,1,260]{2,1,0:T(1,128)S(1)}, u32[]{:S(2)}, u32[]{:S(2)}) async-start(s32[4,1,260]{2,1,0:T(1,128)} %all_to_all.22), calls=%async_computation.1 | async-start | bytes 12288 | tf_op jit(solution)/shard_map/all_to_all | solution.py:97
  31.7 13.2 copy-start.6
  183.0 0.6 copy-start.5
  183.6 99.7 %all-to-all-start.2 = ((f32[4,260,2,8,128]{4,3,2,1,0:T(8,128)}), f32[4,260,2,8,128]{4,3,2,1,0:T(8,128)}, u32[]{:S(2)}, u32[]{:S(2)}) async-start(f32[4,260,2,8,128]{4,3,2,1,0:T(8,128)} %get-tuple-element.363), calls=%async_computation.2 | async-start | bytes 17039360 | tf_op jit(solution)/shard_map/all_to_all | solution.py:103
  189.7 8.1 slice-start
  189.7 8.1 slice-start.1
  189.7 8.1 slice-start.2
  197.8 4.6 copy-start.13
  197.8 4.6 copy-start.14
  197.8 4.6 copy-start.8
  289.7 3.5 copy-start.3
  293.2 2.2 copy-start.4
  298.0 19.7 %copy-start.1 = (f32[128,65,128]{2,0,1:T(8,128)S(1)}, f32[128,65,128]{2,0,1:T(8,128)}, u32[]{:S(2)}) copy-start(f32[128,65,128]{2,0,1:T(8,128)} %get-tuple-element.827) | copy-start | bytes 12779524 | tf_op jit(solution)/shard_map/while
  298.0 19.7 %copy-start.2 = (f32[8,65,2,8,128]{4,3,1,0,2:T(8,128)S(1)}, f32[8,65,2,8,128]{4,3,1,0,2:T(8,128)}, u32[]{:S(2)}) copy-start(f32[8,65,2,8,128]{4,3,1,0,2:T(8,128)} %get-tuple-element.831) | copy-start | bytes 12779524 | tf_op jit(solution)/shard_map/while
  329.5 19.7 %copy-start.1 = (f32[128,65,128]{2,0,1:T(8,128)S(1)}, f32[128,65,128]{2,0,1:T(8,128)}, u32[]{:S(2)}) copy-start(f32[128,65,128]{2,0,1:T(8,128)} %get-tuple-element.827) | copy-start | bytes 12779524 | tf_op jit(solution)/shard_map/while
  329.5 19.7 %copy-start.2 = (f32[8,65,2,8,128]{4,3,1,0,2:T(8,128)S(1)}, f32[8,65,2,8,128]{4,3,1,0,2:T(8,128)}, u32[]{:S(2)}) copy-start(f32[8,65,2,8,128]{4,3,1,0,2:T(8,128)} %get-tuple-element.831) | copy-start | bytes 12779524 | tf_op jit(solution)/shard_map/while
  360.9 19.7 %copy-start.1 = (f32[128,65,128]{2,0,1:T(8,128)S(1)}, f32[128,65,128]{2,0,1:T(8,128)}, u32[]{:S(2)}) copy-start(f32[128,65,128]{2,0,1:T(8,128)} %get-tuple-element.827) | copy-start | bytes 12779524 | tf_op jit(solution)/shard_map/while
  360.9 19.7 %copy-start.2 = (f32[8,65,2,8,128]{4,3,1,0,2:T(8,128)S(1)}, f32[8,65,2,8,128]{4,3,1,0,2:T(8,128)}, u32[]{:S(2)}) copy-start(f32[8,65,2,8,128]{4,3,1,0,2:T(8,128)} %get-tuple-element.831) | copy-start | bytes 12779524 | tf_op jit(solution)/shard_map/while
  392.4 19.7 %copy-start.1 = (f32[128,65,128]{2,0,1:T(8,128)S(1)}, f32[128,65,128]{2,0,1:T(8,128)}, u32[]{:S(2)}) copy-start(f32[128,65,128]{2,0,1:T(8,128)} %get-tuple-element.827) | copy-start | bytes 12779524 | tf_op jit(solution)/shard_map/while
  392.4 19.7 %copy-start.2 = (f32[8,65,2,8,128]{4,3,1,0,2:T(8,128)S(1)}, f32[8,65,2,8,128]{4,3,1,0,2:T(8,128)}, u32[]{:S(2)}) copy-start(f32[8,65,2,8,128]{4,3,1,0,2:T(8,128)} %get-tuple-element.831) | copy-start | bytes 12779524 | tf_op jit(solution)/shard_map/while
  423.8 19.7 %copy-start.1 = (f32[128,65,128]{2,0,1:T(8,128)S(1)}, f32[128,65,128]{2,0,1:T(8,128)}, u32[]{:S(2)}) copy-start(f32[128,65,128]{2,0,1:T(8,128)} %get-tuple-element.827) | copy-start | bytes 12779524 | tf_op jit(solution)/shard_map/while
  423.8 19.7 %copy-start.2 = (f32[8,65,2,8,128]{4,3,1,0,2:T(8,128)S(1)}, f32[8,65,2,8,128]{4,3,1,0,2:T(8,128)}, u32[]{:S(2)}) copy-start(f32[8,65,2,8,128]{4,3,1,0,2:T(8,128)} %get-tuple-element.831) | copy-start | bytes 12779524 | tf_op jit(solution)/shard_map/while
  455.2 19.7 %copy-start.1 = (f32[128,65,128]{2,0,1:T(8,128)S(1)}, f32[128,65,128]{2,0,1:T(8,128)}, u32[]{:S(2)}) copy-start(f32[128,65,128]{2,0,1:T(8,128)} %get-tuple-element.827) | copy-start | bytes 12779524 | tf_op jit(solution)/shard_map/while
  455.2 19.7 %copy-start.2 = (f32[8,65,2,8,128]{4,3,1,0,2:T(8,128)S(1)}, f32[8,65,2,8,128]{4,3,1,0,2:T(8,128)}, u32[]{:S(2)}) copy-start(f32[8,65,2,8,128]{4,3,1,0,2:T(8,128)} %get-tuple-element.831) | copy-start | bytes 12779524 | tf_op jit(solution)/shard_map/while
  486.7 19.7 %copy-start.1 = (f32[128,65,128]{2,0,1:T(8,128)S(1)}, f32[128,65,128]{2,0,1:T(8,128)}, u32[]{:S(2)}) copy-start(f32[128,65,128]{2,0,1:T(8,128)} %get-tuple-element.827) | copy-start | bytes 12779524 | tf_op jit(solution)/shard_map/while
  486.7 19.7 %copy-start.2 = (f32[8,65,2,8,128]{4,3,1,0,2:T(8,128)S(1)}, f32[8,65,2,8,128]{4,3,1,0,2:T(8,128)}, u32[]{:S(2)}) copy-start(f32[8,65,2,8,128]{4,3,1,0,2:T(8,128)} %get-tuple-element.831) | copy-start | bytes 12779524 | tf_op jit(solution)/shard_map/while
  518.1 19.7 %copy-start.1 = (f32[128,65,128]{2,0,1:T(8,128)S(1)}, f32[128,65,128]{2,0,1:T(8,128)}, u32[]{:S(2)}) copy-start(f32[128,65,128]{2,0,1:T(8,128)} %get-tuple-element.827) | copy-start | bytes 12779524 | tf_op jit(solution)/shard_map/while
  518.1 19.7 %copy-start.2 = (f32[8,65,2,8,128]{4,3,1,0,2:T(8,128)S(1)}, f32[8,65,2,8,128]{4,3,1,0,2:T(8,128)}, u32[]{:S(2)}) copy-start(f32[8,65,2,8,128]{4,3,1,0,2:T(8,128)} %get-tuple-element.831) | copy-start | bytes 12779524 | tf_op jit(solution)/shard_map/while
  549.6 19.7 %copy-start.1 = (f32[128,65,128]{2,0,1:T(8,128)S(1)}, f32[128,65,128]{2,0,1:T(8,128)}, u32[]{:S(2)}) copy-start(f32[128,65,128]{2,0,1:T(8,128)} %get-tuple-element.827) | copy-start | bytes 12779524 | tf_op jit(solution)/shard_map/while
  549.6 19.7 %copy-start.2 = (f32[8,65,2,8,128]{4,3,1,0,2:T(8,128)S(1)}, f32[8,65,2,8,128]{4,3,1,0,2:T(8,128)}, u32[]{:S(2)}) copy-start(f32[8,65,2,8,128]{4,3,1,0,2:T(8,128)} %get-tuple-element.831) | copy-start | bytes 12779524 | tf_op jit(solution)/shard_map/while
  662.9 0.6 copy-start.9
  662.9 0.6 copy-start.11
  963.4 3.5 copy-start
  1047.4 131.2 %all-to-all-start.3 = ((f32[4,260,3,8,128]{4,3,2,1,0:T(8,128)}), f32[4,260,3,8,128]{4,3,2,1,0:T(8,128)}, u32[]{:S(2)}, u32[]{:S(2)}) async-start(f32[4,260,3,8,128]{4,3,2,1,0:T(8,128)} %bitcast.196), calls=%async_computation.3 | async-start | bytes 25559040 | tf_op jit(solution)/shard_map/all_to_all | solution.py:154
  1053.7 709.2 %reduce-scatter.2.cloned.1.call-start = ((), (), s32[]{:S(2)}) async-start(), calls=%async_computation.5 | async-start | bytes 28753920 | tf_op jit(solution)/shard_map/reduce_scatter | solution.py:160
  1361.4 8.7 copy-start.7
  1511.6 0.7 copy-start.10
  1511.6 0.7 copy-start.12
Sparse Core Ops, SparseCore 0:
  1511.7 251.2 reduce-scatter.1
where the time goes:
time: 1780 us; the launch traced here: 1770 us
  other arithmetic  533 us (30%)
  waiting for transfers between devices  451 us (25%)
  matrix products  376 us (21%)
  local copies, waits for them, and re-layouts  263 us (15%)
  blocking collectives  77.3 us (4%)
  loops' own time  34 us (2%)
  starting transfers between devices  22 us (1%)
    add x18, other arithmetic, moved_images(): real_part * cosine + imag_part * sine_part  363 us
    reduce_scatter x1, waiting for transfers between devices, shards(): lax.psum_scatter(accumulated, ('orient', 'dp'), scatter_dimension=0, tile...  250 us
    scatter-add x1, other arithmetic, shards(): accumulated.at[cell_index]  142 us
    all_to_all x1, waiting for transfers between devices, shards(): lax.all_to_all(outgoing, 'vol', split_axis=0, concat_axis=0, tiled=True)  125 us
    dot_general x4, matrix products, back_project(): return jnp.einsum('nmkq,nrq->nmkr', tile_rows, matrices, precision=PRECISE)  121 us
    dot_general x9, matrix products, add_step(): jnp.einsum('ikp,itcq->ptckq', share_step, ctf[:, :, None, :] * moved, pre...  92.9 us
    dot_general x9, matrix products, score_step(): jnp.einsum('itcq,ptckq->ikp', ctf_noise[:, :, None, :] * moved, slices, p...  81.5 us
    all_to_all x1, waiting for transfers between devices, shards(): lax.all_to_all(pieces, 'vol', split_axis=0, concat_axis=0, tiled=True)  75.7 us
  transfers between devices with their start and end apart: 5, of which 3 were waited for; matrix products, arithmetic and copies ran while one was open for 2% of the time, Pallas kernels for 0%

commit v1 on v0

v1 whole, which is shorter than its diff:
```python
import math

import jax
import jax.numpy as jnp
import numpy as np
from jax import lax
from jax.experimental import pallas as pl
from jax.experimental.pallas import tpu as pltpu
from jax.sharding import PartitionSpec as P

SIDE = 128
NTRANS = 9
REACH = 3
PREVIOUS_REWARD = 1.5
CHUNK = 8
F32 = jnp.float32
BF16 = jnp.bfloat16


def phase_tables(tile_count, tile_width):
    pixel = np.arange(tile_count * tile_width).reshape(tile_count, tile_width)
    half_width = SIDE // 2 + 1
    freq_x = pixel % half_width
    row = pixel // half_width
    freq_y = np.where(row < SIDE // 2, row, row - SIDE)

    def pair(freq, steps):
        turns = np.mod(freq[:, None, :] * np.asarray(steps)[None, :, None], SIDE)
        angle = turns * (2.0 * math.pi / SIDE)
        return np.concatenate([np.cos(angle), np.sin(angle)], axis=2)

    steps = list(range(-REACH, REACH + 1)) + [0]
    prior = np.concatenate([pair(freq_x, steps), pair(freq_y, steps)], axis=1)
    j = np.arange(NTRANS)
    turns = np.mod(
        freq_x[:, None, :] * (j % 3 - 1)[None, :, None] + freq_y[:, None, :] * (j // 3 - 1)[None, :, None],
        SIDE,
    )
    angle = turns * (2.0 * math.pi / SIDE)
    step = np.stack([np.cos(angle), np.sin(angle)], axis=1)
    return prior.astype(np.float32), step.astype(np.float32)


def divisor(count, most):
    return max(d for d in range(1, most + 1) if count % d == 0)


def split(x):
    high = x.astype(BF16)
    return high, (x - high.astype(F32)).astype(BF16)


def rounded(x):
    high = lax.reduce_precision(x, 8, 7)
    return high.astype(BF16), (x - high).astype(BF16)


def halves_sum(r):
    m, n = r.shape[0] // 2, r.shape[1] // 2
    return (r[:m, :n] + r[m:, :n]) + (r[:m, n:] + r[m:, n:])


def bits_of(count):
    return max(1, (count - 1).bit_length())


def compact(mask, code, spare):
    poses = mask.shape[0]
    order = jnp.arange(poses, dtype=jnp.int32)
    before = (order[:, None] > order[None, :]).astype(BF16)
    rank = jnp.dot(before, mask.astype(BF16), preferred_element_type=F32).astype(jnp.int32)
    rank = jnp.where(mask, rank, -1)
    hit = rank[None, :, :] == order[:, None, None]
    listing = jnp.sum(jnp.where(hit, (code - spare)[None], 0), axis=1) + spare
    return listing.T.reshape(-1), jnp.sum(mask.astype(jnp.int32), axis=0)


def prepare_kernel(x_ref, ctf_ref, pick_x_ref, pick_y_ref, prior_ref, y_ref, square_ref):
    count = x_ref.shape[0]
    width = x_ref.shape[3]
    particles = x_ref.shape[2]
    options = pick_x_ref.shape[1]
    for tt in range(count):
        ex = jnp.dot(pick_x_ref[...], prior_ref[tt, :options], precision=lax.Precision.HIGHEST, preferred_element_type=F32)
        ey = jnp.dot(pick_y_ref[...], prior_ref[tt, options:], precision=lax.Precision.HIGHEST, preferred_element_type=F32)
        cx, sx, cy, sy = ex[:, :width], ex[:, width:], ey[:, :width], ey[:, width:]
        cosine = cx * cy - sx * sy
        sine = sx * cy + cx * sy
        ctf = ctf_ref[tt]
        real, imag = x_ref[tt, 0] * ctf, x_ref[tt, 1] * ctf
        moved = jnp.concatenate([real * cosine + imag * sine, imag * cosine - real * sine], axis=1)
        high, low = split(moved)
        y_ref[tt, :particles, :] = high
        y_ref[tt, particles:, :] = low
        high, low = split(ctf * ctf)
        square_ref[tt, :particles, :] = high
        square_ref[tt, particles:, :] = low


def prepare(x, ctf, pick_x, pick_y, prior, block):
    tiles, _, particles, width = x.shape
    options = pick_x.shape[1]
    return pl.pallas_call(
        prepare_kernel,
        grid=(tiles // block,),
        in_specs=[
            pl.BlockSpec((block, 2, particles, width), lambda t: (t, 0, 0, 0)),
            pl.BlockSpec((block, particles, width), lambda t: (t, 0, 0)),
            pl.BlockSpec((particles, options), lambda t: (0, 0)),
            pl.BlockSpec((particles, options), lambda t: (0, 0)),
            pl.BlockSpec((block, 2 * options, 2 * width), lambda t: (t, 0, 0)),
        ],
        out_specs=[
            pl.BlockSpec((block, 2 * particles, 2 * width), lambda t: (t, 0, 0)),
            pl.BlockSpec((block, 2 * particles, width), lambda t: (t, 0, 0)),
        ],
        out_shape=[
            jax.ShapeDtypeStruct((tiles, 2 * particles, 2 * width), BF16),
            jax.ShapeDtypeStruct((tiles, 2 * particles, width), BF16),
        ],
        compiler_params=pltpu.CompilerParams(vmem_limit_bytes=40 << 20),
        cost_estimate=pl.CostEstimate(flops=tiles * particles * width * 100, bytes_accessed=tiles * particles * width * 24, transcendentals=0),
        name="prepare",
    )(x, ctf, pick_x, pick_y, prior)


NT_DIMS = (((1,), (1,)), ((), ()))


def score_kernel(weight_bits, plane_bits, count_ref, list_ref, volume_ref, weight_ref, y_ref, square_ref, step_ref, noise_ref, out_ref, acc):
    block = pl.program_id(0)
    tiles = y_ref.shape[0]
    width = square_ref.shape[2]
    classes = volume_ref.shape[3]
    poses = out_ref.shape[0]

    @pl.when(block == 0)
    def _():
        acc[...] = jnp.zeros_like(acc)

    def tile(tt, carry):
        t = block * tiles + tt

        def chunk(c, carry):
            pose, real, imag = [], [], []
            for s in range(CHUNK):
                code = list_ref[t * poses + c * CHUNK + s]
                chosen = code & ((1 << weight_bits) - 1)
                plane = (code >> weight_bits) & ((1 << plane_bits) - 1)
                pose.append(code >> (weight_bits + plane_bits))
                high, low = split(volume_ref[plane, tt].reshape(2 * classes, width))
                r = jnp.dot(jnp.concatenate([high, low], axis=0), weight_ref[chosen], preferred_element_type=F32)
                r = halves_sum(r)
                real.append(r[:classes])
                imag.append(r[classes:])
            real, imag = jnp.concatenate(real, axis=0), jnp.concatenate(imag, axis=0)
            noise = noise_ref[tt]
            high, low = split((real * real + imag * imag) * noise)
            r = lax.dot_general(jnp.concatenate([high, low], axis=0), square_ref[tt], NT_DIMS, preferred_element_type=F32)
            norm = halves_sum(r)
            real, imag = real * (2.0 * noise), imag * (2.0 * noise)
            for j in range(NTRANS):
                cosine, sine = step_ref[tt, 0, j : j + 1, :], step_ref[tt, 1, j : j + 1, :]
                turned = jnp.concatenate([real * cosine - imag * sine, real * sine + imag * cosine], axis=1)
                high, low = split(turned)
                r = lax.dot_general(jnp.concatenate([high, low], axis=0), y_ref[tt], NT_DIMS, preferred_element_type=F32)
                r = halves_sum(r) - norm
                n = r.shape[1]
                for s in range(CHUNK):
                    acc[pose[s], :, j * n : (j + 1) * n] += r[s * classes : (s + 1) * classes]
            return carry

        return lax.fori_loop(0, (count_ref[t] + CHUNK - 1) // CHUNK, chunk, carry)

    lax.fori_loop(0, tiles, tile, 0)

    @pl.when(block == pl.num_programs(0) - 1)
    def _():
        out_ref[...] = acc[:poses]


def partial_scores(counts, listing, volume, weights, y, square, step, noise, poses, block):
    planes, tiles, _, classes, width = volume.shape
    particles = y.shape[1] // 2
    bank = weights.shape[0]
    grid_spec = pltpu.PrefetchScalarGridSpec(
        num_scalar_prefetch=2,
        grid=(tiles // block,),
        in_specs=[
            pl.BlockSpec((planes, block, 2, classes, width), lambda t, *_: (0, t, 0, 0, 0)),
            pl.BlockSpec(weights.shape, lambda t, *_: (0, 0, 0), pipeline_mode=pl.Buffered(1)),
            pl.BlockSpec((block, 2 * particles, 2 * width), lambda t, *_: (t, 0, 0)),
            pl.BlockSpec((block, 2 * particles, width), lambda t, *_: (t, 0, 0)),
            pl.BlockSpec((block, 2, NTRANS, width), lambda t, *_: (t, 0, 0, 0)),
            pl.BlockSpec((block, 1, width), lambda t, *_: (t, 0, 0)),
        ],
        out_specs=pl.BlockSpec((poses, classes, NTRANS * particles), lambda t, *_: (0, 0, 0)),
        scratch_shapes=[pltpu.VMEM((poses + 1, classes, NTRANS * particles), F32)],
    )

    def body(*refs):
        score_kernel(bits_of(bank), bits_of(planes), *refs)

    return pl.pallas_call(
        body,
        grid_spec=grid_spec,
        out_shape=jax.ShapeDtypeStruct((poses, classes, NTRANS * particles), F32),
        compiler_params=pltpu.CompilerParams(vmem_limit_bytes=56 << 20),
        name="score",
    )(counts, listing, volume, weights, y, square, step, noise)


def spread_kernel(weight_bits, plane_bits, count_ref, list_ref, score_ref, term_ref, weight_ref, y_ref, square_ref, step_ref,
                  own_ref, other_ref, posterior_ref, evidence_ref, share, acc):
    block = pl.program_id(0)
    tiles = y_ref.shape[0]
    width = square_ref.shape[2]
    poses, classes = score_ref.shape[0], score_ref.shape[1]
    n = term_ref.shape[1]
    half = own_ref.shape[0]

    @pl.when(block == 0)
    def _():
        term = term_ref[...]

        def largest(p, best):
            for j in range(NTRANS):
                best = jnp.maximum(best, score_ref[p, :, j * n : (j + 1) * n] + term)
            return best

        best = lax.fori_loop(0, poses, largest, jnp.full((classes, n), -jnp.inf, F32))
        peak = jnp.max(best, axis=0, keepdims=True)

        def mass(p, total):
            for j in range(NTRANS):
                total = total + jnp.exp((score_ref[p, :, j * n : (j + 1) * n] + term) - peak)
            return total

        class_mass = lax.fori_loop(0, poses, mass, jnp.zeros((classes, n), F32))
        total = jnp.sum(class_mass, axis=0, keepdims=True)
        posterior_ref[...] = class_mass / total
        evidence_ref[...] = peak + jnp.log(total)
        factor = jnp.broadcast_to(poses / total, (classes, n))

        def normal(p, carry):
            every = jnp.zeros((classes, n), F32)
            for j in range(NTRANS):
                e = jnp.exp((score_ref[p, :, j * n : (j + 1) * n] + term) - peak) * factor
                every = every + e
                high = e.astype(BF16).astype(F32)
                share[p, :, j * n : (j + 1) * n] = jnp.concatenate([high, e - high], axis=0).astype(BF16)
            high = every.astype(BF16).astype(F32)
            share[p, :, NTRANS * n :] = jnp.concatenate([high, every - high], axis=0).astype(BF16)
            return carry

        lax.fori_loop(0, poses, normal, 0)

    def pairs(r):
        return [r[2 * s * classes : (2 * s + 1) * classes] + r[(2 * s + 1) * classes : (2 * s + 2) * classes] for s in range(CHUNK)]

    def tile(tt, carry):
        t = block * tiles + tt
        acc[...] = jnp.zeros_like(acc)

        def chunk(c, carry):
            pose, plane, chosen = [], [], []
            for s in range(CHUNK):
                code = list_ref[t * poses + c * CHUNK + s]
                chosen.append(code & ((1 << weight_bits) - 1))
                plane.append((code >> weight_bits) & ((1 << plane_bits) - 1))
                pose.append(code >> (weight_bits + plane_bits))
            real = jnp.zeros((CHUNK * classes, width), F32)
            imag = jnp.zeros((CHUNK * classes, width), F32)
            for j in range(NTRANS):
                rows = jnp.concatenate([share[pose[s], :, j * n : (j + 1) * n] for s in range(CHUNK)], axis=0)
                r = jnp.dot(jnp.concatenate([rows, rows], axis=1), y_ref[tt], preferred_element_type=F32)
                r = jnp.concatenate(pairs(r), axis=0)
                cosine, sine = step_ref[tt, 0, j : j + 1, :], step_ref[tt, 1, j : j + 1, :]
                real = real + (r[:, :width] * cosine + r[:, width:] * sine)
                imag = imag + (r[:, width:] * cosine - r[:, :width] * sine)
            rows = jnp.concatenate([share[pose[s], :, NTRANS * n :] for s in range(CHUNK)], axis=0)
            r = jnp.dot(jnp.concatenate([rows, rows], axis=1), square_ref[tt], preferred_element_type=F32)
            power = pairs(r)
            for s in range(CHUNK):
                where = slice(s * classes, (s + 1) * classes)
                rows = jnp.concatenate([real[where], imag[where], power[s]], axis=0)
                high = rows.astype(BF16).astype(F32)
                both = jnp.concatenate([high, rows - high], axis=0).astype(BF16)
                r = jnp.dot(both, weight_ref[chosen[s]], preferred_element_type=F32)
                acc[plane[s]] += halves_sum(r)
            return carry

        lax.fori_loop(0, (count_ref[t] + CHUNK - 1) // CHUNK, chunk, 0)
        own_ref[:, tt] = acc[:half].reshape(half, 3, classes, width)
        other_ref[:, tt] = acc[half : 2 * half].reshape(half, 3, classes, width)
        return carry

    lax.fori_loop(0, tiles, tile, 0)


def spread(counts, listing, scores, term, weights, y, square, step, planes, block):
    poses, classes, _ = scores.shape
    tiles, particles, width = square.shape[0], square.shape[1] // 2, square.shape[2]
    bank = weights.shape[0]
    half = planes // 2
    part = pl.BlockSpec((half, block, 3, classes, width), lambda t, *_: (0, t, 0, 0, 0))
    grid_spec = pltpu.PrefetchScalarGridSpec(
        num_scalar_prefetch=2,
        grid=(tiles // block,),
        in_specs=[
            pl.BlockSpec(scores.shape, lambda t, *_: (0, 0, 0), pipeline_mode=pl.Buffered(1)),
            pl.BlockSpec(term.shape, lambda t, *_: (0, 0)),
            pl.BlockSpec(weights.shape, lambda t, *_: (0, 0, 0), pipeline_mode=pl.Buffered(1)),
            pl.BlockSpec((block, 2 * particles, 2 * width), lambda t, *_: (t, 0, 0)),
            pl.BlockSpec((block, 2 * particles, width), lambda t, *_: (t, 0, 0)),
            pl.BlockSpec((block, 2, NTRANS, width), lambda t, *_: (t, 0, 0, 0)),
        ],
        out_specs=[part, part, pl.BlockSpec((classes, particles), lambda t, *_: (0, 0)), pl.BlockSpec((1, particles), lambda t, *_: (0, 0))],
        scratch_shapes=[
            pltpu.VMEM((poses, 2 * classes, (NTRANS + 1) * particles), BF16),
            pltpu.VMEM((planes + 1, 3 * classes, width), F32),
        ],
    )

    def body(*refs):
        spread_kernel(bits_of(bank), bits_of(planes + 1), *refs)

    shape = jax.ShapeDtypeStruct((half, tiles, 3, classes, width), F32)
    return pl.pallas_call(
        body,
        grid_spec=grid_spec,
        out_shape=[shape, shape, jax.ShapeDtypeStruct((classes, particles), F32), jax.ShapeDtypeStruct((1, particles), F32)],
        compiler_params=pltpu.CompilerParams(vmem_limit_bytes=58 << 20),
        name="spread",
    )(counts, listing, scores, term, weights, y, square, step)


def shards(volume, weight_bank, tile_slab, tile_plane, tile_weight, particles, ctf, noise_weight, offsets, earlier_class, pose_free_term):
    slabs, orients, parts = lax.axis_size("vol"), lax.axis_size("orient"), lax.axis_size("dp")
    slab, orient, part = lax.axis_index("vol"), lax.axis_index("orient"), lax.axis_index("dp")
    planes, tiles, _, classes, width = volume.shape
    bank = weight_bank.shape[0]
    local_poses = tile_plane.shape[0]
    group = slabs * local_poses
    block = divisor(tiles, 5)

    named = jnp.stack([tile_slab[:, :, 0], tile_plane, tile_weight])
    named = lax.all_gather(named, ("vol", "orient"))

    prior, step = phase_tables(tiles, width)
    options = prior.shape[1] // 2
    pick = [(offsets[:, axis : axis + 1] + REACH == jnp.arange(options, dtype=jnp.int32)[None]).astype(F32) for axis in (0, 1)]
    y, square = prepare(particles.transpose(1, 2, 0, 3), ctf.transpose(1, 0, 2), pick[0], pick[1], prior, block)
    high, low = rounded(weight_bank)
    ahead = jnp.concatenate([high, low], axis=2)
    high, low = rounded(weight_bank.transpose(0, 2, 1))
    back = jnp.concatenate([high, low], axis=2)

    weight_bits = bits_of(bank)
    named = named.reshape(slabs, orients, 3, local_poses, tiles)
    own = lax.dynamic_index_in_dim(named, orient, axis=1, keepdims=False)
    own = own.transpose(1, 0, 2, 3).reshape(3, group, tiles)
    pose = jnp.arange(group, dtype=jnp.int32)[:, None]
    shift = weight_bits + bits_of(planes)
    code = (pose << shift) | (own[1] << weight_bits) | own[2]
    listing, counts = compact(own[0] == slab, code, group << shift)

    every = named.transpose(2, 0, 1, 3, 4).reshape(3, slabs * orients * local_poses, tiles)
    reach = planes // orients
    half = reach // parts
    pose = jnp.arange(every.shape[1], dtype=jnp.int32)[:, None]
    place = jnp.mod(every[1] - orient * reach - part * half, reach)
    shift = weight_bits + bits_of(reach + 1)
    code = (pose << shift) | (place << weight_bits) | every[2]
    mask = (every[0] == slab) & (every[1] // reach == orient)
    back_listing, back_counts = compact(mask, code, reach << weight_bits)

    scores = partial_scores(counts, listing, volume, ahead, y, square, step, noise_weight[:, None, :], group, block)
    scores = lax.psum_scatter(scores, "vol", scatter_dimension=0, tiled=True)
    scores = lax.all_gather(scores, ("vol", "orient"), tiled=True)

    term = jnp.where(earlier_class[None, :] == jnp.arange(classes, dtype=jnp.int32)[:, None], PREVIOUS_REWARD, 0.0)
    term = term + pose_free_term[None, :]
    mine, other, posterior, evidence = spread(back_counts, back_listing, scores, term, back, y, square, step, reach, block)
    numerator = mine + lax.ppermute(other, "dp", [(0, 1), (1, 0)])
    return numerator, posterior.T, evidence[0]


def solution(mesh):
    in_specs = (
        P("vol", None, None, None, None),
        P(),
        P(("vol", "orient"), None, None),
        P(("vol", "orient"), None),
        P(("vol", "orient"), None),
        P("dp", None, None, None),
        P("dp", None, None),
        P(),
        P("dp", None),
        P("dp"),
        P("dp"),
    )
    out_specs = (P(("vol", "orient", "dp"), None, None, None, None), P("dp", None), P("dp"))
    return jax.shard_map(shards, mesh=mesh, in_specs=in_specs, out_specs=out_specs, check_vma=False)
```

time: 1780 us -> 429 us (0.24)
  other arithmetic: 533 us -> 19.6 us
  matrix products: 376 us -> 0.29 us
  waiting for transfers between devices: 451 us -> 98.1 us
  local copies, waits for them, and re-layouts: 263 us -> 17.4 us
  Pallas kernels: 0 us -> 232 us
  loops' own time: 34 us -> 0 us
  blocking collectives: 77.3 us -> 44.1 us
  starting transfers between devices: 22 us -> 0.11 us
    dot_general x28 -> x2, matrix products: 376 us -> 0.29 us  [compact(): jnp.dot(before, mask.astype(BF16), preferred_element_type=F32)]
    add x39 -> x3, other arithmetic: 365 us -> 4.61 us  [the longest x1 4.01 us: shards(): numerator = mine + lax.ppermute(other, 'dp', [(0, 1), (1, 0)])]
    pallas_call x0 -> x3, Pallas kernels: none -> 232 us  [the longest x1 120 us: partial_scores(): pl.pallas_call(body, grid_spec=grid_spec, out_shape=jax.ShapeDtypeStruct(...]
    reduce_scatter x1, waiting for transfers between devices: 250 us -> 24.6 us  [shards(): scores = lax.psum_scatter(scores, 'vol', scatter_dimension=0, tiled=True)]
    all_to_all x4 -> x0, waiting for transfers between devices: 200 us -> none  [the longest x1 125 us: shards(): lax.all_to_all(outgoing, 'vol', split_axis=0, concat_axis=0, tiled=True)]
    scatter-add x1 -> x0, other arithmetic: 142 us -> none  [shards(): accumulated.at[cell_index]]
    gather x10 -> x0, local copies, waits for them, and re-layouts: 137 us -> none  [the longest x4 58.9 us: back_project(): matrices = weight_bank[chosen]]
    scatter x3 -> x0, local copies, waits for them, and re-layouts: 77.7 us -> none  [the longest x1 69.5 us: shards(): outgoing.at[slot_index]]
  transfers between devices with their start and end apart: 5 -> 3, of which waited for: 3 -> 3; matrix products, arithmetic and copies ran while one was open for 2% -> 4% of each run, Pallas kernels for 0% -> 0%
where the time goes in v1:
time: 429 us; the launch traced here: 426 us
  Pallas kernels  232 us (54%)
  waiting for transfers between devices  98.1 us (23%)
  blocking collectives  44.1 us (10%)
  other arithmetic  19.6 us (5%)
  local copies, waits for them, and re-layouts  17.4 us (4%)
  between operations  14.2 us (3%)
    pallas_call x1, Pallas kernels, partial_scores(): pl.pallas_call(body, grid_spec=grid_spec, out_shape=jax.ShapeDtypeStruct(...  120 us
    pallas_call x1, Pallas kernels, spread(): pl.pallas_call(body, grid_spec=grid_spec, out_shape=[shape, shape, jax.Sh...  94.2 us
    all_gather x1, waiting for transfers between devices, shards(): scores = lax.all_gather(scores, ('vol', 'orient'), tiled=True)  67.6 us
    all_gather x1, blocking collectives, shards(): named = lax.all_gather(named, ('vol', 'orient'))  44.1 us
    reduce_scatter x1, waiting for transfers between devices, shards(): scores = lax.psum_scatter(scores, 'vol', scatter_dimension=0, tiled=True)  24.6 us
    pallas_call x1, Pallas kernels, prepare(): pl.pallas_call(prepare_kernel, grid=(tiles // block,), in_specs=[pl.Block...  18.4 us
    unnamed x18, local copies, waits for them, and re-layouts  15.7 us
  transfers between devices with their start and end apart: 3, of which 3 were waited for; matrix products, arithmetic and copies ran while one was open for 4% of the time, Pallas kernels for 0%

profile of v1, /device:TPU:0, one launch (start us, length us, event | category | flops | bytes accessed | tf_op | source)
XLA Modules:
  0.0 426.3 jit_solution(5480308990864546278)
XLA Ops:
  7.2 0.0 reduce-scatter.2.cloned.1.call-start
  7.2 0.7 pad_add_fusion
  8.0 44.1 %all-gather = s32[48,8,65]{2,1,0:T(8,128)S(1)} all-gather(s32[3,8,65]{2,1,0:T(8,128)S(1)} %pad_add_fusion), channel_id=2, replica_groups=mesh['vol'=4,'orient'=4,'dp'=2] {'vol','orient'}, dimensions={0}, use_global_device_ids=true | all-gather | bytes 106080 | tf_op jit(solution)/shard_map/all_gather | solution.py:348
  52.1 0.5 convert_reduce_fusion.1
  52.6 0.1 fusion.3
  52.8 0.1 fusion.26
  52.8 0.1 select_reduce_fusion.1
  52.9 0.1 copy.57
  53.0 0.7 reshape.112.refs_1_
  53.7 0.8 add_bitcast_fusion.2
  54.5 8.1 %copy.63 = f32[128,65,2,128]{3,0,2,1:T(8,128)} copy(f32[128,65,2,128]{3,2,1,0:T(2,128)} %param.18) | data formatting | bytes 17039360 | tf_op args[5]
  62.6 0.0 copy-done.2
  62.6 1.2 reduce-precision_convert_fusion.1
  63.8 0.0 copy-done.3
  63.8 0.6 broadcast_in_dim.63.refs_7_
  64.4 0.1 fusion.7
  64.5 0.0 copy-start.1
  64.5 2.7 pad_maximum_fusion.refs_3_
  67.2 0.0 slice-done
  67.2 0.0 slice-done.1
  67.2 0.0 copy-done.1
  67.2 18.4 %prepare.1 = (bf16[65,256,256]{2,1,0:T(8,128)(2,1)}, bf16[65,256,128]{2,1,0:T(8,128)(2,1)S(1)}) custom-call(f32[65,2,128,128]{3,2,1,0:T(8,128)} %bitcast.51, f32[65,128,128]{2,1,0:T(8,128)S(1)} %bitcast.50, f32[128,8]{1,0:T(8,128)S(1)} %get-tuple-element.29.pick_x_ref, f32[128,8]{1,0:T(8,128)S(1)} %get-tuple-element.30.pick_y_ref, f32[65,16,256]{2,1,0:T(8,128)S(1)} %copy-done.1), custom_call_target="tpu_custom_call" | custom-call | flops 106496000 | bytes 25559040 | tf_op jit(solution)/shard_map/prepare/pallas_call | solution.py:103
  85.6 2.0 copy-done
  87.6 119.9 %score.1 = f32[32,8,1152]{2,1,0:T(8,128)} custom-call(s32[65]{0:T(128)} %get-tuple-element.15.refs_0_, s32[2080]{0:T(1024)} %reshape.112.refs_1_, f32[32,65,2,8,128]{4,3,2,1,0:T(8,128)} %refs_2_.1, bf16[64,128,256]{2,1,0:T(8,128)(2,1)} %pad_maximum_fusion.refs_3_, bf16[65,256,256]{2,1,0:T(8,128)(2,1)} %get-tuple-element.9.refs_4_.refs_5_, ...), custom_call_target="tpu_custom_call" | custom-call | tf_op jit(solution)/shard_map/score/pallas_call | solution.py:204
  207.4 0.0 reduce-scatter.2.cloned.1.call-update
  207.5 0.0 all-gather.3.cloned.1.call-start
  207.5 24.6 %reduce-scatter.2.cloned.1.call-done = f32[8,8,1152]{2,1,0:T(8,128)} async-done(((f32[32,8,1152]{2,1,0:T(8,128)}), f32[8,8,1152]{2,1,0:T(8,128)}) %reduce-scatter.2.cloned.1.call-update) | async-done | bytes 294928 | tf_op jit(solution)/shard_map/reduce_scatter | solution.py:379
  232.1 0.0 all-gather.3.cloned.1.call-update
  232.1 5.6 %copy.59 = f32[64,128,128]{1,2,0:T(8,128)} copy(f32[64,128,128]{2,1,0:T(8,128)} %param.14) | data formatting | bytes 8388608 | tf_op args[1]
  237.7 0.6 fusion.35
  238.4 0.1 copy.49
  238.5 0.1 copy.55
  238.6 0.1 copy.53
  238.7 0.2 fusion.2
  238.9 1.5 select_reduce_fusion
  240.4 3.4 reduce-precision_convert_fusion
  243.8 0.0 copy-start.4
  243.8 0.0 copy-start.5
  243.8 2.7 pad_maximum_fusion.1.refs_4_
  246.5 0.0 copy-done.4
  246.5 0.0 copy-done.5
  246.5 0.6 select_add_fusion.refs_3_
  247.1 0.6 add_bitcast_fusion.refs_1_
  247.7 67.6 %all-gather.3.cloned.1.call-done.refs_2_ = f32[128,8,1152]{2,1,0:T(8,128)} async-done(((f32[8,8,1152]{2,1,0:T(8,128)}), f32[128,8,1152]{2,1,0:T(8,128)}) %all-gather.3.cloned.1.call-update) | async-done | bytes 4718608 | tf_op jit(solution)/shard_map/all_gather | solution.py:380
  315.3 94.2 %spread.1 = (f32[4,65,3,8,128]{4,3,2,1,0:T(8,128)}, f32[4,65,3,8,128]{4,3,2,1,0:T(8,128)}, f32[8,128]{1,0:T(8,128)}, f32[1,128]{1,0:T(1,128)}) custom-call(s32[65]{0:T(128)} %get-tuple-element.25.refs_0_, s32[8320]{0:T(1024)} %add_bitcast_fusion.refs_1_, f32[128,8,1152]{2,1,0:T(8,128)} %all-gather.3.cloned.1.call-done.refs_2_, ...), custom_call_target="tpu_custom_call" | custom-call | tf_op jit(solution)/shard_map/spread/pallas_call | solution.py:329
  409.5 0.0 collective-permute-start
  409.5 5.9 %collective-permute-done = f32[4,65,3,8,128]{4,3,2,1,0:T(8,128)S(1)} collective-permute-done((f32[4,65,3,8,128]{4,3,2,1,0:T(8,128)}, f32[4,65,3,8,128]{4,3,2,1,0:T(8,128)S(1)}, u32[]{:S(2)}, u32[]{:S(2)}) %collective-permute-start) | collective-permute-done | bytes 3194912 | tf_op jit(solution)/shard_map/ppermute | solution.py:385
  415.4 4.0 add.69
  (12 shorter events, 0.1 us)
Async XLA Ops:
  7.2 224.9 %reduce-scatter.2.cloned.1.call-start = ((), (), s32[]{:S(2)}) async-start(), calls=%async_computation.1 | async-start | bytes 1474560 | tf_op jit(solution)/shard_map/reduce_scatter | solution.py:379
  54.5 8.1 %copy-start.2 = (f32[64,128,128]{2,1,0:T(8,128)S(1)}, f32[64,128,128]{2,1,0:T(8,128)}, u32[]{:S(2)}) copy-start(f32[64,128,128]{2,1,0:T(8,128)} %param.14) | copy-start | bytes 12582916
  62.6 1.2 copy-start.3
  62.6 4.6 %slice-start = ((s8[4259840]{0:T(1024)(128)(4,1)}), s8[4194304]{0:T(1024)(128)(4,1)S(1)}, s32[]{:S(2)}) async-start(s8[4259840]{0:T(1024)(128)(4,1)} %bitcast.48), calls=%async_computation.3 | async-start | bytes 8388608
  64.4 2.8 slice-start.1
  64.5 2.7 copy-start.1
  85.6 2.0 copy-start
  207.5 107.8 %all-gather.3.cloned.1.call-start = ((), (), s32[]{:S(2)}) async-start(), calls=%async_computation.2 | async-start | bytes 5013504 | tf_op jit(solution)/shard_map/all_gather | solution.py:380
  243.8 2.7 copy-start.4
  243.8 2.7 copy-start.5
  409.5 6.0 %collective-permute-start = (f32[4,65,3,8,128]{4,3,2,1,0:T(8,128)}, f32[4,65,3,8,128]{4,3,2,1,0:T(8,128)S(1)}, u32[]{:S(2)}, u32[]{:S(2)}) collective-permute-start(f32[4,65,3,8,128]{4,3,2,1,0:T(8,128)} %get-tuple-element.12), channel_id=1, source_target_pairs={{0,1},{1,0},{2,3},{3,2},{4,5},{5,4},{6,7},{7,6},{8,9},{9,8},{10,11... | collective-permute-start | bytes 9584648 | tf_op jit(solution)/shard_map/ppermute | solution.py:385
Sparse Core Ops, SparseCore 0:
  207.6 24.4 reduce-scatter.1
  234.8 80.4 all-gather.2
